TPU v7x, 256 devices: a whole 4x4x8 slice. The times are simulated.
256 devices in a mesh: section: 2 (over core), seq: 16 (over x, y), tensor: 8 (over z).
Axes of the slice: x: 4, y: 4, z: 8, core: 2. Of those that a mesh axis runs over, the one named last changes fastest.
Arguments:
- x_in: bfloat16 [2, 32768, 2048], P(None, 'seq', 'tensor'), may hold values from -6 to 6
- norm_gain: float32 [2, 2048], P('section', 'tensor'), may hold values from 0.5 to 1.5
- right_blocks: bfloat16 [2, 128, 256, 256], P('section', 'seq'), may hold values from -0.375 to 0.375
- left_blocks: bfloat16 [2, 256, 128, 128], P('section', 'seq'), may hold values from -0.5 to 0.5
- gate_first: bfloat16 [2, 32, 64, 64], P('section'), may hold values from -0.75 to 0.75
- gate_second: bfloat16 [2, 64, 32, 32], P('section'), may hold values from -1 to 1
- out_first: bfloat16 [2, 32, 64, 64], P('section'), may hold values from -0.75 to 0.75
- out_second: bfloat16 [2, 64, 32, 32], P('section'), may hold values from -1 to 1
- head: bfloat16 [2, 2048, 32768], P('section', None, ('seq', 'tensor')), may hold values from -0.375 to 0.375
- targets: int32 [2, 256], replicated, may hold values from 0 to 32767
Outputs:
- block_out: bfloat16 [2, 2, 32768, 2048], P('section', None, 'seq', 'tensor')
- aux_losses: float32 [2, 2, 256], P('section')
All inputs are finite; a program needn't handle non-finite values.
Results may differ from a plain program's by a relative error of at most 0.011.
Values may be sent and summed in bfloat16 or wider, within the bound.
No kernel may reach another device: no remote copies, remote signals or barrier semaphores. Data moves between devices by JAX's collectives and lax.ppermute only.
A program may use at most 128 MiB of HBM per device.

v0:
```python
import jax
import jax.numpy as jnp
from jax import lax
from jax.sharding import PartitionSpec as P

C1 = 32
C2 = 64
D = 2048
STRIDE = 128
epsilon = 1e-05


def from_behind(block, axis, distance):
    devices = range(lax.axis_size(axis))
    route = [(i - distance, i) for i in devices if i - distance in devices]
    return lax.ppermute(block, axis, route)


def first_map(factor_local):
    c_one, c_two, _ = factor_local.shape
    identity = jnp.eye(c_one, dtype=factor_local.dtype)
    dense_map = identity[None, :, :, None] * jnp.transpose(factor_local, (1, 0, 2))[:, :, None, :]
    return dense_map.reshape(c_two * c_one, c_one * c_two)


def second_map(factor_local, groups, c_one):
    k_dev = factor_local.shape[0]
    split_view = factor_local.reshape(k_dev, groups, c_one, groups, c_one)
    split_view = jnp.transpose(split_view, (1, 2, 0, 3, 4))
    identity = jnp.eye(k_dev, dtype=factor_local.dtype)
    dense_map = split_view[:, :, :, :, None, :] * identity[None, None, :, None, :, None]
    return dense_map.reshape(groups * c_one * k_dev, groups * k_dev * c_one)


def restore_rows(returned, groups, c_one, k_dev, token_count):
    ordered = returned.reshape(groups, c_one, k_dev, token_count)
    return jnp.transpose(ordered, (3, 1, 0, 2)).reshape(token_count, c_one * groups * k_dev)


def gate_channels(normed, one_map, two_map, groups, c_one, k_dev):
    token_count = normed.shape[0]
    first_mix = jnp.einsum("oc,tc->ot", one_map, normed, preferred_element_type=jnp.float32).astype(
        jnp.bfloat16
    )
    first_mix = first_mix.reshape(groups, k_dev * c_one, token_count)
    incoming = lax.all_to_all(first_mix, "tensor", split_axis=0, concat_axis=0, tiled=True)
    count_here = incoming.shape[2]
    flat_in = incoming.reshape(groups * k_dev * c_one, count_here)
    second_mix = jnp.dot(two_map, flat_in, preferred_element_type=jnp.float32).astype(jnp.bfloat16)
    returned = lax.all_to_all(
        second_mix.reshape(groups, c_one * k_dev, count_here),
        "tensor",
        split_axis=0,
        concat_axis=0,
        tiled=True,
    )
    return restore_rows(returned, groups, c_one, k_dev, token_count)


def out_channels(values, one_map, two_map, groups, c_one, k_dev):
    token_count = values.shape[0]
    first_mix = jnp.einsum("oc,tc->ot", one_map, values, preferred_element_type=jnp.float32).astype(
        jnp.bfloat16
    )
    first_mix = first_mix.reshape(groups, k_dev * c_one, token_count)
    incoming = lax.all_to_all(first_mix, "tensor", split_axis=0, concat_axis=0, tiled=True)
    count_here = incoming.shape[2]
    flat_in = incoming.reshape(groups * k_dev * c_one, count_here)
    second_mix = jnp.dot(two_map, flat_in, preferred_element_type=jnp.float32).astype(jnp.bfloat16)
    returned = lax.all_to_all(
        second_mix.reshape(groups, c_one * k_dev, count_here),
        "tensor",
        split_axis=0,
        concat_axis=0,
        tiled=True,
    )
    return restore_rows(returned, groups, c_one, k_dev, token_count)


def sequence_mix(normed, right_local, left_local, row_count, col_count):
    chan_count = normed.shape[1]
    seq_view = normed.reshape(row_count, col_count, chan_count)
    row_mix = jnp.einsum(
        "pjq,pqc->pjc", right_local, seq_view, preferred_element_type=jnp.float32
    ).astype(jnp.bfloat16)
    col_mix = jnp.einsum(
        "jip,pjc->ijc",
        left_local,
        lax.all_to_all(row_mix, "seq", split_axis=1, concat_axis=0, tiled=True),
        preferred_element_type=jnp.float32,
    ).astype(jnp.bfloat16)
    returned = lax.all_to_all(col_mix, "seq", split_axis=0, concat_axis=1, tiled=True)
    return returned.reshape(row_count * col_count, chan_count)


def body(
    x_in,
    norm_gain,
    right_blocks,
    left_blocks,
    gate_first,
    gate_second,
    out_first,
    out_second,
    head,
    targets,
):
    section_index = lax.axis_index("section")
    tensor_count = lax.axis_size("tensor")
    tensor_index = lax.axis_index("tensor")
    micro_count = x_in.shape[0]
    tok_dev = x_in.shape[1]
    chan_dev = x_in.shape[2]
    row_count = right_blocks.shape[1]
    col_count = right_blocks.shape[2]
    c_one = C1 // tensor_count
    k_dev = C2 // tensor_count
    norm_scale = norm_gain[0]
    right_local = right_blocks[0]
    left_local = left_blocks[0]
    gate_first_all = gate_first[0]
    gate_second_all = gate_second[0]
    out_first_all = out_first[0]
    out_second_all = out_second[0]
    gate_one = first_map(lax.dynamic_slice_in_dim(gate_first_all, tensor_index * c_one, c_one, 0))
    gate_two = second_map(
        lax.dynamic_slice_in_dim(gate_second_all, tensor_index * k_dev, k_dev, 0),
        tensor_count,
        c_one,
    )
    out_one = first_map(lax.dynamic_slice_in_dim(out_first_all, tensor_index * c_one, c_one, 0))
    out_two = second_map(
        lax.dynamic_slice_in_dim(out_second_all, tensor_index * k_dev, k_dev, 0),
        tensor_count,
        c_one,
    )
    head_local = head[0]
    vocab_dev = head_local.shape[1]
    vocab_offset = lax.axis_index(("seq", "tensor")) * vocab_dev
    handed = jnp.zeros((tok_dev, chan_dev), jnp.bfloat16)
    first_outputs, second_outputs, first_losses, second_losses = ([], [], [], [])
    for step_index in range(micro_count + 1):
        feed_rows = x_in[min(step_index, micro_count - 1)]
        x_val = jnp.where(section_index == 0, feed_rows, handed)
        labels = jnp.where(
            section_index == 0,
            targets[min(step_index, micro_count - 1)],
            targets[max(step_index - 1, 0)],
        )
        x_float = x_val.astype(jnp.float32)
        square_part = jnp.sum(x_float * x_float, axis=1)
        square_total = lax.psum(square_part, "tensor")
        row_scale = lax.rsqrt(square_total / D + epsilon)
        normed = (x_float * row_scale[:, None] * norm_scale[None, :]).astype(jnp.bfloat16)
        seq_out = sequence_mix(normed, right_local, left_local, row_count, col_count)
        gate_pre = gate_channels(normed, gate_one, gate_two, tensor_count, c_one, k_dev)
        gated_mix = (
            seq_out.astype(jnp.float32) * jax.nn.sigmoid(gate_pre.astype(jnp.float32))
        ).astype(jnp.bfloat16)
        out_pre = out_channels(gated_mix, out_one, out_two, tensor_count, c_one, k_dev)
        result = (x_float + out_pre.astype(jnp.float32)).astype(jnp.bfloat16)
        scored = result.reshape(row_count, col_count, chan_dev)[:, ::STRIDE, :].reshape(
            -1, chan_dev
        )
        wide_rows = lax.all_gather(scored, "tensor", axis=1, tiled=True)
        logits = jnp.dot(
            lax.all_gather(wide_rows, "seq", axis=0, tiled=True),
            head_local,
            preferred_element_type=jnp.float32,
        )
        exp_sums = jnp.sum(jnp.exp(logits), axis=1)
        vocab_ids = jnp.arange(vocab_dev, dtype=jnp.int32)[None, :] + vocab_offset
        is_target = vocab_ids == labels[:, None]
        target_part = jnp.sum(jnp.where(is_target, logits, 0.0), axis=1)
        exp_total, target_logit = lax.psum((exp_sums, target_part), ("seq", "tensor"))
        result, aux_loss = (result, jnp.log(exp_total) - target_logit)
        if step_index < micro_count:
            first_outputs.append(result)
            first_losses.append(aux_loss)
            handed = from_behind(result, "section", 1)
        if step_index > 0:
            second_outputs.append(result)
            second_losses.append(aux_loss)
    block_out = jnp.where(section_index == 0, jnp.stack(first_outputs), jnp.stack(second_outputs))[
        None
    ]
    aux_losses = jnp.where(section_index == 0, jnp.stack(first_losses), jnp.stack(second_losses))[
        None
    ]
    return (block_out, aux_losses)


def solution(mesh):
    in_specs = (
        P(None, "seq", "tensor"),
        P("section", "tensor"),
        P("section", "seq", None, None),
        P("section", "seq", None, None),
        P("section", None, None, None),
        P("section", None, None, None),
        P("section", None, None, None),
        P("section", None, None, None),
        P("section", None, ("seq", "tensor")),
        P(),
    )
    out_specs = (P("section", None, "seq", "tensor"), P("section", None, None))
    return jax.shard_map(body, mesh=mesh, in_specs=in_specs, out_specs=out_specs, check_vma=False)
```

profile of v0, /device:TPU:0, one launch (start us, length us, event | category | flops | bytes accessed | tf_op | source)
XLA Modules:
  0.0 1093.3 jit_solution(17827740526057056564)
XLA Ops:
  9.6 2.7 fusion.55
  13.2 18.5 %psum.63 = f32[2048]{0:T(1024)S(1)} all-reduce(f32[2048]{0:T(1024)S(1)} %fusion.18), channel_id=1, replica_groups=mesh['section'=2,'seq'=16,'tensor'=8] {'tensor'}, use_global_device_ids=true, to_apply=%region_1.2 | all-reduce | flops 2048 | bytes 16384 | tf_op jit(solution)/shard_map/psum | solution.py:152
  33.3 4.2 all-to-all-start.2
  40.4 2.7 copy.92
  43.1 19.9 %all-to-all-done.2 = bf16[8,32,2048]{2,1,0:T(8,128)(2,1)} async-done(((bf16[8,32,2048]{2,1,0:T(8,128)(2,1)}), bf16[8,32,2048]{2,1,0:T(8,128)(2,1)}, u32[]{:S(2)}, u32[]{:S(2)}) %all-to-all-start.2) | async-done | bytes 1048608 | tf_op jit(solution)/shard_map/all_to_all | solution.py:46
  63.0 7.1 all-to-all-start
  70.7 2.8 broadcast_multiply_fusion
  73.5 2.8 mul.233
  76.4 2.7 convolution_convert_fusion.10
  79.0 5.0 all-to-all-done
  84.0 3.7 all-to-all-start.3
  90.7 2.7 copy.96
  93.4 17.9 %all-to-all-done.3 = bf16[8,32,2048]{2,1,0:T(8,128)(2,1)S(1)} async-done(((bf16[8,32,2048]{2,1,0:T(8,128)(2,1)}), bf16[8,32,2048]{2,1,0:T(8,128)(2,1)S(1)}, u32[]{:S(2)}, u32[]{:S(2)}) %all-to-all-start.3) | async-done | bytes 1048608 | tf_op jit(solution)/shard_map/all_to_all | solution.py:50
  111.3 5.0 all-to-all-start.1
  117.2 9.1 reshape.474
  126.3 11.8 %copy.100 = f32[8,16,16,256]{3,2,0,1:T(8,128)S(1)} copy(f32[8,16,16,256]{2,1,0,3:T(8,128)} %reshape.474) | data formatting | bytes 4194304 | tf_op jit(solution)/shard_map/div | solution.py:158
  141.2 4.2 all-to-all-start.4
  145.4 2.9 mul.218
  148.3 22.9 %all-to-all-done.4 = bf16[8,32,2048]{2,1,0:T(8,128)(2,1)} async-done(((bf16[8,32,2048]{2,1,0:T(8,128)(2,1)}), bf16[8,32,2048]{2,1,0:T(8,128)(2,1)}, u32[]{:S(2)}, u32[]{:S(2)}) %all-to-all-start.4) | async-done | bytes 1048608 | tf_op jit(solution)/shard_map/all_to_all | solution.py:66
  172.9 28.1 %all_to_all.141 = bf16[8,32,2048]{2,1,0:T(8,128)(2,1)S(1)} all-to-all(bf16[8,32,2048]{2,1,0:T(8,128)(2,1)S(1)} %bitcast.255), channel_id=1, replica_groups=mesh['section'=2,'seq'=16,'tensor'=8] {'tensor'}, dimensions={0} | all-to-all | bytes 2097152 | tf_op jit(solution)/shard_map/all_to_all | solution.py:70
  208.3 2.7 fusion
  211.0 14.9 %psum.64 = f32[2048]{0:T(1024)S(1)} all-reduce(f32[2048]{0:T(1024)S(1)} %get-tuple-element.22), channel_id=1, replica_groups=mesh['section'=2,'seq'=16,'tensor'=8] {'tensor'}, use_global_device_ids=true, to_apply=%region_3.4 | all-reduce | flops 2048 | bytes 16384 | tf_op jit(solution)/shard_map/psum | solution.py:152
  229.9 4.2 all-to-all-start.8
  234.2 2.7 fusion.20
  236.9 2.6 copy.106
  239.5 20.1 %all-to-all-done.8 = bf16[8,32,2048]{2,1,0:T(8,128)(2,1)} async-done(((bf16[8,32,2048]{2,1,0:T(8,128)(2,1)}), bf16[8,32,2048]{2,1,0:T(8,128)(2,1)}, u32[]{:S(2)}, u32[]{:S(2)}) %all-to-all-start.8) | async-done | bytes 1048608 | tf_op jit(solution)/shard_map/all_to_all | solution.py:46
  259.6 7.0 all-to-all-start.6
  266.6 2.7 convolution_convert_fusion.6
  269.3 11.2 %all-to-all-done.6 = bf16[8,256,256]{2,0,1:T(8,128)(2,1)} async-done(((bf16[8,256,256]{2,0,1:T(8,128)(2,1)}), bf16[8,256,256]{2,0,1:T(8,128)(2,1)}, u32[]{:S(2)}, u32[]{:S(2)}) %all-to-all-start.6) | async-done | bytes 1048608 | tf_op jit(solution)/shard_map/all_to_all | solution.py:89
  280.5 4.2 all-to-all-start.9
  287.8 2.7 copy.110
  290.5 17.9 %all-to-all-done.9 = bf16[8,32,2048]{2,1,0:T(8,128)(2,1)} async-done(((bf16[8,32,2048]{2,1,0:T(8,128)(2,1)}), bf16[8,32,2048]{2,1,0:T(8,128)(2,1)}, u32[]{:S(2)}, u32[]{:S(2)}) %all-to-all-start.9) | async-done | bytes 1048608 | tf_op jit(solution)/shard_map/all_to_all | solution.py:50
  308.4 4.7 all-to-all-start.7
  316.3 10.4 reshape.479
  326.8 12.9 %copy.112 = f32[8,16,16,256]{3,2,0,1:T(8,128)} copy(f32[8,16,16,256]{2,1,0,3:T(8,128)} %reshape.479) | data formatting | bytes 4194304 | tf_op jit(solution)/shard_map/div | solution.py:158
  342.4 28.1 %all_to_all.142 = bf16[8,32,2048]{2,1,0:T(8,128)(2,1)S(1)} all-to-all(bf16[8,32,2048]{2,1,0:T(8,128)(2,1)S(1)} %bitcast.258), channel_id=1, replica_groups=mesh['section'=2,'seq'=16,'tensor'=8] {'tensor'}, dimensions={0} | all-to-all | bytes 2097152 | tf_op jit(solution)/shard_map/all_to_all | solution.py:66
  371.0 27.4 %all_to_all.143 = bf16[8,32,2048]{2,1,0:T(8,128)(2,1)S(1)} all-to-all(bf16[8,32,2048]{2,1,0:T(8,128)(2,1)S(1)} %bitcast.260), channel_id=1, replica_groups=mesh['section'=2,'seq'=16,'tensor'=8] {'tensor'}, dimensions={0} | all-to-all | bytes 2097152 | tf_op jit(solution)/shard_map/all_to_all | solution.py:70
  405.1 15.0 %psum.65 = f32[2048]{0:T(1024)S(1)} all-reduce(f32[2048]{0:T(1024)S(1)} %get-tuple-element.20), channel_id=1, replica_groups=mesh['section'=2,'seq'=16,'tensor'=8] {'tensor'}, use_global_device_ids=true, to_apply=%region_5.6 | all-reduce | flops 2048 | bytes 16384 | tf_op jit(solution)/shard_map/psum | solution.py:152
  424.1 4.2 all-to-all-start.14
  428.3 2.7 fusion.21
  431.0 2.6 copy.116
  433.7 20.5 %all-to-all-done.14 = bf16[8,32,2048]{2,1,0:T(8,128)(2,1)} async-done(((bf16[8,32,2048]{2,1,0:T(8,128)(2,1)}), bf16[8,32,2048]{2,1,0:T(8,128)(2,1)}, u32[]{:S(2)}, u32[]{:S(2)}) %all-to-all-start.14) | async-done | bytes 1048608 | tf_op jit(solution)/shard_map/all_to_all | solution.py:46
  454.1 6.9 all-to-all-start.12
  461.0 2.7 convolution_convert_fusion.2
  463.7 11.3 %all-to-all-done.12 = bf16[8,256,256]{2,0,1:T(8,128)(2,1)} async-done(((bf16[8,256,256]{2,0,1:T(8,128)(2,1)}), bf16[8,256,256]{2,0,1:T(8,128)(2,1)}, u32[]{:S(2)}, u32[]{:S(2)}) %all-to-all-start.12) | async-done | bytes 1048608 | tf_op jit(solution)/shard_map/all_to_all | solution.py:89
  474.9 4.2 all-to-all-start.15
  482.2 2.7 copy.120
  484.9 18.1 %all-to-all-done.15 = bf16[8,32,2048]{2,1,0:T(8,128)(2,1)} async-done(((bf16[8,32,2048]{2,1,0:T(8,128)(2,1)}), bf16[8,32,2048]{2,1,0:T(8,128)(2,1)}, u32[]{:S(2)}, u32[]{:S(2)}) %all-to-all-start.15) | async-done | bytes 1048608 | tf_op jit(solution)/shard_map/all_to_all | solution.py:50
  503.0 4.7 all-to-all-start.13
  511.0 10.4 reshape.483
  521.4 12.9 %copy.122 = f32[8,16,16,256]{3,2,0,1:T(8,128)} copy(f32[8,16,16,256]{2,1,0,3:T(8,128)} %reshape.483) | data formatting | bytes 4194304 | tf_op jit(solution)/shard_map/div | solution.py:158
  538.1 4.3 all-to-all-start.16
  545.2 6.3 slice.28
  553.0 32.3 %all_gather.18 = bf16[16,2048]{1,0:T(8,128)(2,1)} all-gather(bf16[16,256]{1,0:T(8,128)(2,1)S(1)} %reshape.465), channel_id=1, replica_groups=mesh['section'=2,'seq'=16,'tensor'=8] {'tensor'}, dimensions={1}, use_global_device_ids=true | all-gather | bytes 73728 | tf_op jit(solution)/shard_map/all_gather | solution.py:165
  585.3 2.7 convolution_convert_fusion
  587.9 5.8 all-to-all-start.17
  597.3 35.3 %all_gather.20 = bf16[16,2048]{1,0:T(8,128)(2,1)} all-gather(bf16[16,256]{1,0:T(8,128)(2,1)S(1)} %reshape.467), channel_id=1, replica_groups=mesh['section'=2,'seq'=16,'tensor'=8] {'tensor'}, dimensions={1}, use_global_device_ids=true | all-gather | bytes 73728 | tf_op jit(solution)/shard_map/all_gather | solution.py:165
  640.3 26.5 %all_gather.22 = bf16[16,2048]{1,0:T(8,128)(2,1)} all-gather(bf16[16,256]{1,0:T(8,128)(2,1)S(1)} %reshape.469), channel_id=1, replica_groups=mesh['section'=2,'seq'=16,'tensor'=8] {'tensor'}, dimensions={1}, use_global_device_ids=true | all-gather | bytes 73728 | tf_op jit(solution)/shard_map/all_gather | solution.py:165
  666.9 2.5 fusion.27
  671.7 11.2 %all-gather.6.cloned.1.call-done = bf16[256,2048]{1,0:T(8,128)(2,1)} async-done(((bf16[16,2048]{1,0:T(8,128)(2,1)}), bf16[256,2048]{1,0:T(8,128)(2,1)}) %all-gather.6.cloned.1.call-update) | async-done | bytes 1048592 | tf_op jit(solution)/shard_map/all_gather | solution.py:167
  682.9 2.9 fusion.34
  687.4 4.0 copy.129
  691.5 40.9 %all-gather.8.cloned.1.call-done = bf16[256,2048]{1,0:T(8,128)(2,1)} async-done(((bf16[16,2048]{1,0:T(8,128)(2,1)}), bf16[256,2048]{1,0:T(8,128)(2,1)}) %all-gather.8.cloned.1.call-update) | async-done | bytes 1048592 | tf_op jit(solution)/shard_map/all_gather | solution.py:167
  734.2 351.8 %all-reduce = (f32[256]{0:T(256)S(1)}, f32[256]{0:T(256)S(1)}, f32[256]{0:T(256)S(1)}, f32[256]{0:T(256)S(1)}, f32[256]{0:T(256)S(1)}, /*index=5*/f32[256]{0:T(256)S(1)}) all-reduce(f32[256]{0:T(256)S(1)} %get-tuple-element.30, f32[256]{0:T(256)S(1)} %get-tuple-element.31, ...), channel_id=1, replica_groups=mesh['section'=2,'seq'=16,'tensor'=8] {'seq','tensor'}, use_global_device_ids=true, to_apply=%region_13.14 | all-reduce | flops 1536 | bytes 12288 | tf_op jit(solution)/shard_map/psum | solution.py:175
  (152 shorter events, 80.2 us)
Async XLA Ops:
  7.2 31.8 %copy-start = (bf16[1,8,256,256]{3,2,1,0:T(8,128)(2,1)S(1)}, bf16[1,8,256,256]{3,2,1,0:T(8,128)(2,1)}, u32[]{:S(2)}) copy-start(bf16[1,8,256,256]{3,2,1,0:T(8,128)(2,1)} %param.12) | copy-start | bytes 3145732
  9.5 22.2 %copy-start.19 = (bf16[256,256]{1,0:T(8,128)(2,1)}, bf16[256,256]{1,0:T(8,128)(2,1)S(1)}, u32[]{:S(2)}) copy-start(bf16[256,256]{1,0:T(8,128)(2,1)S(1)} %mul.236) | copy-start | bytes 393220
  12.3 19.5 %copy-start.26 = (f32[1,256]{1,0:T(1,128)S(1)}, f32[1,256]{1,0:T(1,128)}, u32[]{:S(2)}) copy-start(f32[1,256]{1,0:T(1,128)} %param.11) | copy-start | bytes 3076
  12.9 24.6 %copy-start.1 = (bf16[1,2048,256]{1,2,0:T(8,128)(2,1)}, bf16[1,2048,256]{1,2,0:T(8,128)(2,1)S(1)}, u32[]{:S(2)}) copy-start(bf16[1,2048,256]{1,2,0:T(8,128)(2,1)S(1)} %copy.135) | copy-start | bytes 3145732
  33.3 29.7 %all-to-all-start.2 = ((bf16[8,32,2048]{2,1,0:T(8,128)(2,1)}), bf16[8,32,2048]{2,1,0:T(8,128)(2,1)}, u32[]{:S(2)}, u32[]{:S(2)}) async-start(bf16[8,32,2048]{2,1,0:T(8,128)(2,1)} %bitcast.21), calls=%async_computation.2 | async-start | bytes 2097152 | tf_op jit(solution)/shard_map/all_to_all | solution.py:46
  38.6 1.8 copy-start.3
  40.4 29.7 %copy-start.24 = (bf16[1,64,32,32]{1,3,2,0:T(8,128)(2,1)S(1)}, bf16[1,64,32,32]{1,3,2,0:T(8,128)(2,1)}, u32[]{:S(2)}) copy-start(bf16[1,64,32,32]{1,3,2,0:T(8,128)(2,1)} %param.15) | copy-start | bytes 393220
  43.1 27.0 %copy-start.25 = (bf16[1,64,32,32]{1,3,2,0:T(8,128)(2,1)S(1)}, bf16[1,64,32,32]{1,3,2,0:T(8,128)(2,1)}, u32[]{:S(2)}) copy-start(bf16[1,64,32,32]{1,3,2,0:T(8,128)(2,1)} %param.17) | copy-start | bytes 393220
  63.0 21.0 %all-to-all-start = ((bf16[8,256,256]{2,0,1:T(8,128)(2,1)}), bf16[8,256,256]{2,0,1:T(8,128)(2,1)}, u32[]{:S(2)}, u32[]{:S(2)}) async-start(bf16[8,256,256]{2,0,1:T(8,128)(2,1)} %copy.92), calls=%async_computation | async-start | bytes 2097152 | tf_op jit(solution)/shard_map/all_to_all | solution.py:89
  84.0 5.2 copy-start.14
  84.0 27.3 %all-to-all-start.3 = ((bf16[8,32,2048]{2,1,0:T(8,128)(2,1)}), bf16[8,32,2048]{2,1,0:T(8,128)(2,1)S(1)}, u32[]{:S(2)}, u32[]{:S(2)}) async-start(bf16[8,32,2048]{2,1,0:T(8,128)(2,1)} %bitcast.247), calls=%async_computation.3 | async-start | bytes 2097152 | tf_op jit(solution)/shard_map/all_to_all | solution.py:50
  90.7 25.6 %copy-start.22 = (bf16[64,4,4,64]{3,2,1,0:T(4,128)(2,1)S(1)}, bf16[64,4,4,64]{3,2,1,0:T(4,128)(2,1)}, u32[]{:S(2)}) copy-start(bf16[64,4,4,64]{3,2,1,0:T(4,128)(2,1)} %get-tuple-element.35) | copy-start | bytes 393220
  111.3 26.8 %all-to-all-start.1 = ((bf16[128,16,256]{2,1,0:T(8,128)(2,1)}), bf16[128,16,256]{2,1,0:T(8,128)(2,1)}, u32[]{:S(2)}, u32[]{:S(2)}) async-start(bf16[128,16,256]{2,1,0:T(8,128)(2,1)} %copy.96), calls=%async_computation.1 | async-start | bytes 2097152 | tf_op jit(solution)/shard_map/all_to_all | solution.py:92
  139.7 5.7 copy-start.13
  141.2 30.0 %all-to-all-start.4 = ((bf16[8,32,2048]{2,1,0:T(8,128)(2,1)}), bf16[8,32,2048]{2,1,0:T(8,128)(2,1)}, u32[]{:S(2)}, u32[]{:S(2)}) async-start(bf16[8,32,2048]{2,1,0:T(8,128)(2,1)} %bitcast.250), calls=%async_computation.4 | async-start | bytes 2097152 | tf_op jit(solution)/shard_map/all_to_all | solution.py:66
  201.2 1.2 copy-start.2
  203.7 4.6 collective-permute-start
  225.9 2.5 copy-start.20
  227.5 1.0 copy-start.6
  229.9 29.7 %all-to-all-start.8 = ((bf16[8,32,2048]{2,1,0:T(8,128)(2,1)}), bf16[8,32,2048]{2,1,0:T(8,128)(2,1)}, u32[]{:S(2)}, u32[]{:S(2)}) async-start(bf16[8,32,2048]{2,1,0:T(8,128)(2,1)} %bitcast.251), calls=%async_computation.8 | async-start | bytes 2097152 | tf_op jit(solution)/shard_map/all_to_all | solution.py:46
  259.6 20.8 %all-to-all-start.6 = ((bf16[8,256,256]{2,0,1:T(8,128)(2,1)}), bf16[8,256,256]{2,0,1:T(8,128)(2,1)}, u32[]{:S(2)}, u32[]{:S(2)}) async-start(bf16[8,256,256]{2,0,1:T(8,128)(2,1)} %copy.106), calls=%async_computation.6 | async-start | bytes 2097152 | tf_op jit(solution)/shard_map/all_to_all | solution.py:89
  280.5 27.9 %all-to-all-start.9 = ((bf16[8,32,2048]{2,1,0:T(8,128)(2,1)}), bf16[8,32,2048]{2,1,0:T(8,128)(2,1)}, u32[]{:S(2)}, u32[]{:S(2)}) async-start(bf16[8,32,2048]{2,1,0:T(8,128)(2,1)} %bitcast.248), calls=%async_computation.9 | async-start | bytes 2097152 | tf_op jit(solution)/shard_map/all_to_all | solution.py:50
  284.7 1.6 copy-start.15
  308.4 31.3 %all-to-all-start.7 = ((bf16[128,16,256]{2,1,0:T(8,128)(2,1)}), bf16[128,16,256]{2,1,0:T(8,128)(2,1)}, u32[]{:S(2)}, u32[]{:S(2)}) async-start(bf16[128,16,256]{2,1,0:T(8,128)(2,1)} %copy.110), calls=%async_computation.7 | async-start | bytes 2097152 | tf_op jit(solution)/shard_map/all_to_all | solution.py:92
  398.6 1.2 copy-start.9
  399.8 3.9 copy-start.7
  400.1 5.0 copy-start.10
  400.1 3.6 collective-permute-start.1
  420.1 2.5 copy-start.21
  421.7 1.0 copy-start.5
  424.1 30.1 %all-to-all-start.14 = ((bf16[8,32,2048]{2,1,0:T(8,128)(2,1)}), bf16[8,32,2048]{2,1,0:T(8,128)(2,1)}, u32[]{:S(2)}, u32[]{:S(2)}) async-start(bf16[8,32,2048]{2,1,0:T(8,128)(2,1)} %bitcast.249), calls=%async_computation.14 | async-start | bytes 2097152 | tf_op jit(solution)/shard_map/all_to_all | solution.py:46
  454.1 20.8 %all-to-all-start.12 = ((bf16[8,256,256]{2,0,1:T(8,128)(2,1)}), bf16[8,256,256]{2,0,1:T(8,128)(2,1)}, u32[]{:S(2)}, u32[]{:S(2)}) async-start(bf16[8,256,256]{2,0,1:T(8,128)(2,1)} %copy.116), calls=%async_computation.12 | async-start | bytes 2097152 | tf_op jit(solution)/shard_map/all_to_all | solution.py:89
  474.9 28.1 %all-to-all-start.15 = ((bf16[8,32,2048]{2,1,0:T(8,128)(2,1)}), bf16[8,32,2048]{2,1,0:T(8,128)(2,1)}, u32[]{:S(2)}, u32[]{:S(2)}) async-start(bf16[8,32,2048]{2,1,0:T(8,128)(2,1)} %bitcast.246), calls=%async_computation.15 | async-start | bytes 2097152 | tf_op jit(solution)/shard_map/all_to_all | solution.py:50
  479.2 1.6 copy-start.16
  503.0 31.3 %all-to-all-start.13 = ((bf16[128,16,256]{2,1,0:T(8,128)(2,1)}), bf16[128,16,256]{2,1,0:T(8,128)(2,1)}, u32[]{:S(2)}, u32[]{:S(2)}) async-start(bf16[128,16,256]{2,1,0:T(8,128)(2,1)} %copy.120), calls=%async_computation.13 | async-start | bytes 2097152 | tf_op jit(solution)/shard_map/all_to_all | solution.py:92
  538.1 47.2 %all-to-all-start.16 = ((bf16[8,32,2048]{2,1,0:T(8,128)(2,1)}), bf16[8,32,2048]{2,1,0:T(8,128)(2,1)}, u32[]{:S(2)}, u32[]{:S(2)}) async-start(bf16[8,32,2048]{2,1,0:T(8,128)(2,1)} %bitcast.244), calls=%async_computation.16 | async-start | bytes 2097152 | tf_op jit(solution)/shard_map/all_to_all | solution.py:66
  542.3 127.1 %all-gather.4.cloned.1.call-start = ((), (), s32[]{:S(2)}) async-start(), calls=%async_computation.18 | async-start | bytes 1114112 | tf_op jit(solution)/shard_map/all_gather | solution.py:167
  542.4 1.6 copy-start.4
  587.9 44.8 %all-to-all-start.17 = ((bf16[8,32,2048]{2,1,0:T(8,128)(2,1)}), bf16[8,32,2048]{2,1,0:T(8,128)(2,1)}, u32[]{:S(2)}, u32[]{:S(2)}) async-start(bf16[8,32,2048]{2,1,0:T(8,128)(2,1)} %bitcast.245), calls=%async_computation.17 | async-start | bytes 2097152 | tf_op jit(solution)/shard_map/all_to_all | solution.py:70
  593.7 89.2 %all-gather.6.cloned.1.call-start = ((), (), s32[]{:S(2)}) async-start(), calls=%async_computation.19 | async-start | bytes 1114112 | tf_op jit(solution)/shard_map/all_gather | solution.py:167
  632.7 99.7 %all-gather.8.cloned.1.call-start = ((), (), s32[]{:S(2)}) async-start(), calls=%async_computation.20 | async-start | bytes 1114112 | tf_op jit(solution)/shard_map/all_gather | solution.py:167
  634.2 1.2 copy-start.8
  636.7 30.1 %copy-start.27 = (s32[2,256]{1,0:T(2,128)S(1)}, s32[2,256]{1,0:T(2,128)}, u32[]{:S(2)}) copy-start(s32[2,256]{1,0:T(2,128)} %param.19) | copy-start | bytes 6148
  669.4 16.4 %copy-start.11 = (bf16[2048,256]{0,1:T(8,128)(2,1)S(1)}, bf16[2048,256]{0,1:T(8,128)(2,1)}, u32[]{:S(2)}) copy-start(bf16[2048,256]{0,1:T(8,128)(2,1)} %copy-done.10) | copy-start | bytes 3145732
  669.4 16.4 %copy-start.12 = (bf16[2048,256]{0,1:T(8,128)(2,1)S(1)}, bf16[2048,256]{0,1:T(8,128)(2,1)}, u32[]{:S(2)}) copy-start(bf16[2048,256]{0,1:T(8,128)(2,1)} %fusion.7) | copy-start | bytes 3145732
  682.9 2.9 copy-start.18
  687.4 44.9 %copy-start.17 = (bf16[1,2048,256]{2,1,0:T(8,128)(2,1)S(1)}, bf16[1,2048,256]{2,1,0:T(8,128)(2,1)}, u32[]{:S(2)}) copy-start(bf16[1,2048,256]{2,1,0:T(8,128)(2,1)} %param.18) | copy-start | bytes 3145732
  687.4 44.9 %copy-start.23 = (f32[256,256]{0,1:T(8,128)S(1)}, f32[256,256]{0,1:T(8,128)}, u32[]{:S(2)}) copy-start(f32[256,256]{0,1:T(8,128)} %fusion.34) | copy-start | bytes 786436
Sparse Core Ops, SparseCore 0:
  585.4 47.9 all-gather.3
  635.8 47.0 all-gather.5
  685.3 47.0 all-gather.7
where the time goes:
time: 1100 us; the launch traced here: 1090 us
  blocking collectives  578 us (53%)
  waiting for transfers between devices  219 us (20%)
  local copies, waits for them, and re-layouts  132 us (12%)
  starting transfers between devices  78.2 us (7%)
  matrix products  38.8 us (4%)
  other arithmetic  32.9 us (3%)
  between operations  14.8 us (1%)
    psum x1, blocking collectives, body(): lax.psum((exp_sums, target_part), ('seq', 'tensor'))  352 us
    all_gather x3, blocking collectives, body(): wide_rows = lax.all_gather(scored, 'tensor', axis=1, tiled=True)  94.1 us
    div x9, local copies, waits for them, and re-layouts, body(): jax.nn.sigmoid(gate_pre.astype(jnp.float32))  70.5 us
    all_to_all x3, waiting for transfers between devices, gate_channels(): lax.all_to_all(first_mix, 'tensor', split_axis=0, concat_axis=0, tiled=True)  60.5 us
    all_to_all x2, blocking collectives, out_channels(): lax.all_to_all(second_mix.reshape(groups, c_one * k_dev, count_here), 'te...  55.5 us
    all_to_all x3, waiting for transfers between devices, gate_channels(): lax.all_to_all(second_mix.reshape(groups, c_one * k_dev, count_here), 'te...  53.8 us
    all_gather x3, waiting for transfers between devices, body(): lax.all_gather(wide_rows, 'seq', axis=0, tiled=True)  52.1 us
    psum x3, blocking collectives, body(): square_total = lax.psum(square_part, 'tensor')  48.4 us
  transfers between devices with their start and end apart: 20, of which 13 were waited for; matrix products, arithmetic and copies ran while one was open for 15% of the time, Pallas kernels for 0%

commit v1 on v0

--- a/solution.py
+++ b/solution.py
@@ -172,7 +172,7 @@
         vocab_ids = jnp.arange(vocab_dev, dtype=jnp.int32)[None, :] + vocab_offset
         is_target = vocab_ids == labels[:, None]
         target_part = jnp.sum(jnp.where(is_target, logits, 0.0), axis=1)
-        exp_total, target_logit = lax.psum((exp_sums, target_part), ("seq", "tensor"))
+        exp_total, target_logit = lax.psum(lax.psum((exp_sums, target_part), "tensor"), "seq")
         result, aux_loss = (result, jnp.log(exp_total) - target_logit)
         if step_index < micro_count:
             first_outputs.append(result)

time: 1100 us -> 809 us (0.74)
  blocking collectives: 578 us -> 282 us
    psum x1 -> x2, blocking collectives: 352 us -> 56.3 us  [the longest x1 38.6 us: body(): lax.psum(lax.psum((exp_sums, target_part), 'tensor'), 'seq')]
  transfers between devices with their start and end apart: 20 -> 20, of which waited for: 13 -> 13; matrix products, arithmetic and copies ran while one was open for 15% -> 20% of each run, Pallas kernels for 0% -> 0%
where the time goes in v1:
time: 809 us; the launch traced here: 798 us
  blocking collectives  282 us (35%)
  waiting for transfers between devices  220 us (27%)
  local copies, waits for them, and re-layouts  132 us (16%)
  starting transfers between devices  78.2 us (10%)
  matrix products  38.8 us (5%)
  other arithmetic  32.8 us (4%)
  between operations  14.8 us (2%)
    all_gather x3, blocking collectives, body(): wide_rows = lax.all_gather(scored, 'tensor', axis=1, tiled=True)  93.8 us
    div x9, local copies, waits for them, and re-layouts, body(): jax.nn.sigmoid(gate_pre.astype(jnp.float32))  70.5 us
    all_to_all x3, waiting for transfers between devices, gate_channels(): lax.all_to_all(first_mix, 'tensor', split_axis=0, concat_axis=0, tiled=True)  60.6 us
    all_to_all x2, blocking collectives, out_channels(): lax.all_to_all(second_mix.reshape(groups, c_one * k_dev, count_here), 'te...  55.5 us
    all_to_all x3, waiting for transfers between devices, gate_channels(): lax.all_to_all(second_mix.reshape(groups, c_one * k_dev, count_here), 'te...  53.8 us
    all_gather x3, waiting for transfers between devices, body(): lax.all_gather(wide_rows, 'seq', axis=0, tiled=True)  52.5 us
    psum x3, blocking collectives, body(): square_total = lax.psum(square_part, 'tensor')  48.4 us
    psum x1, blocking collectives, body(): lax.psum(lax.psum((exp_sums, target_part), 'tensor'), 'seq')  38.6 us
  transfers between devices with their start and end apart: 20, of which 13 were waited for; matrix products, arithmetic and copies ran while one was open for 20% of the time, Pallas kernels for 0%

profile of v1, /device:TPU:0, one launch (start us, length us, event | category | flops | bytes accessed | tf_op | source)
XLA Modules:
  0.0 797.8 jit_solution(1722624848958694534)
XLA Ops:
  9.6 2.7 fusion.55
  13.2 18.5 %psum.105 = f32[2048]{0:T(1024)S(1)} all-reduce(f32[2048]{0:T(1024)S(1)} %fusion.18), channel_id=1, replica_groups=mesh['section'=2,'seq'=16,'tensor'=8] {'tensor'}, use_global_device_ids=true, to_apply=%region_1.2 | all-reduce | flops 2048 | bytes 16384 | tf_op jit(solution)/shard_map/psum | solution.py:152
  33.3 4.2 all-to-all-start.2
  40.4 2.7 copy.92
  43.1 19.9 %all-to-all-done.2 = bf16[8,32,2048]{2,1,0:T(8,128)(2,1)} async-done(((bf16[8,32,2048]{2,1,0:T(8,128)(2,1)}), bf16[8,32,2048]{2,1,0:T(8,128)(2,1)}, u32[]{:S(2)}, u32[]{:S(2)}) %all-to-all-start.2) | async-done | bytes 1048608 | tf_op jit(solution)/shard_map/all_to_all | solution.py:46
  63.0 7.1 all-to-all-start
  70.6 2.8 broadcast_multiply_fusion
  73.5 2.8 mul.233
  76.3 2.7 convolution_convert_fusion.10
  79.0 5.0 all-to-all-done
  84.0 3.7 all-to-all-start.3
  90.7 2.7 copy.96
  93.4 17.9 %all-to-all-done.3 = bf16[8,32,2048]{2,1,0:T(8,128)(2,1)S(1)} async-done(((bf16[8,32,2048]{2,1,0:T(8,128)(2,1)}), bf16[8,32,2048]{2,1,0:T(8,128)(2,1)S(1)}, u32[]{:S(2)}, u32[]{:S(2)}) %all-to-all-start.3) | async-done | bytes 1048608 | tf_op jit(solution)/shard_map/all_to_all | solution.py:50
  111.2 5.0 all-to-all-start.1
  117.2 9.1 %reshape.474 = f32[8,16,16,256]{2,1,0,3:T(8,128)} reshape(f32[2048,4,8,8]{0,3,2,1:T(8,128)S(1)} %copy.99) | data formatting | bytes 4194304 | tf_op jit(solution)/shard_map/div | solution.py:158
  126.2 11.8 %copy.100 = f32[8,16,16,256]{3,2,0,1:T(8,128)S(1)} copy(f32[8,16,16,256]{2,1,0,3:T(8,128)} %reshape.474) | data formatting | bytes 4194304 | tf_op jit(solution)/shard_map/div | solution.py:158
  141.1 4.2 all-to-all-start.4
  145.4 2.9 mul.218
  148.3 22.9 %all-to-all-done.4 = bf16[8,32,2048]{2,1,0:T(8,128)(2,1)} async-done(((bf16[8,32,2048]{2,1,0:T(8,128)(2,1)}), bf16[8,32,2048]{2,1,0:T(8,128)(2,1)}, u32[]{:S(2)}, u32[]{:S(2)}) %all-to-all-start.4) | async-done | bytes 1048608 | tf_op jit(solution)/shard_map/all_to_all | solution.py:66
  172.8 28.1 %all_to_all.141 = bf16[8,32,2048]{2,1,0:T(8,128)(2,1)S(1)} all-to-all(bf16[8,32,2048]{2,1,0:T(8,128)(2,1)S(1)} %bitcast.255), channel_id=1, replica_groups=mesh['section'=2,'seq'=16,'tensor'=8] {'tensor'}, dimensions={0} | all-to-all | bytes 2097152 | tf_op jit(solution)/shard_map/all_to_all | solution.py:70
  208.2 2.7 fusion
  210.9 14.9 %psum.106 = f32[2048]{0:T(1024)S(1)} all-reduce(f32[2048]{0:T(1024)S(1)} %get-tuple-element.28), channel_id=1, replica_groups=mesh['section'=2,'seq'=16,'tensor'=8] {'tensor'}, use_global_device_ids=true, to_apply=%region_3.4 | all-reduce | flops 2048 | bytes 16384 | tf_op jit(solution)/shard_map/psum | solution.py:152
  229.8 4.2 all-to-all-start.8
  234.0 2.7 fusion.20
  236.7 2.6 copy.106
  239.4 20.2 %all-to-all-done.8 = bf16[8,32,2048]{2,1,0:T(8,128)(2,1)} async-done(((bf16[8,32,2048]{2,1,0:T(8,128)(2,1)}), bf16[8,32,2048]{2,1,0:T(8,128)(2,1)}, u32[]{:S(2)}, u32[]{:S(2)}) %all-to-all-start.8) | async-done | bytes 1048608 | tf_op jit(solution)/shard_map/all_to_all | solution.py:46
  259.6 7.0 all-to-all-start.6
  266.5 2.7 convolution_convert_fusion.6
  269.2 11.2 %all-to-all-done.6 = bf16[8,256,256]{2,0,1:T(8,128)(2,1)} async-done(((bf16[8,256,256]{2,0,1:T(8,128)(2,1)}), bf16[8,256,256]{2,0,1:T(8,128)(2,1)}, u32[]{:S(2)}, u32[]{:S(2)}) %all-to-all-start.6) | async-done | bytes 1048608 | tf_op jit(solution)/shard_map/all_to_all | solution.py:89
  280.4 4.2 all-to-all-start.9
  287.7 2.7 copy.110
  290.4 17.9 %all-to-all-done.9 = bf16[8,32,2048]{2,1,0:T(8,128)(2,1)} async-done(((bf16[8,32,2048]{2,1,0:T(8,128)(2,1)}), bf16[8,32,2048]{2,1,0:T(8,128)(2,1)}, u32[]{:S(2)}, u32[]{:S(2)}) %all-to-all-start.9) | async-done | bytes 1048608 | tf_op jit(solution)/shard_map/all_to_all | solution.py:50
  308.3 4.7 all-to-all-start.7
  316.2 10.4 %reshape.479 = f32[8,16,16,256]{2,1,0,3:T(8,128)} reshape(f32[2048,4,8,8]{0,3,2,1:T(8,128)} %copy.111) | data formatting | bytes 4194304 | tf_op jit(solution)/shard_map/div | solution.py:158
  326.7 12.9 %copy.112 = f32[8,16,16,256]{3,2,0,1:T(8,128)} copy(f32[8,16,16,256]{2,1,0,3:T(8,128)} %reshape.479) | data formatting | bytes 4194304 | tf_op jit(solution)/shard_map/div | solution.py:158
  342.3 28.1 %all_to_all.142 = bf16[8,32,2048]{2,1,0:T(8,128)(2,1)S(1)} all-to-all(bf16[8,32,2048]{2,1,0:T(8,128)(2,1)S(1)} %bitcast.258), channel_id=1, replica_groups=mesh['section'=2,'seq'=16,'tensor'=8] {'tensor'}, dimensions={0} | all-to-all | bytes 2097152 | tf_op jit(solution)/shard_map/all_to_all | solution.py:66
  370.9 27.4 %all_to_all.143 = bf16[8,32,2048]{2,1,0:T(8,128)(2,1)S(1)} all-to-all(bf16[8,32,2048]{2,1,0:T(8,128)(2,1)S(1)} %bitcast.260), channel_id=1, replica_groups=mesh['section'=2,'seq'=16,'tensor'=8] {'tensor'}, dimensions={0} | all-to-all | bytes 2097152 | tf_op jit(solution)/shard_map/all_to_all | solution.py:70
  405.0 15.0 %psum.107 = f32[2048]{0:T(1024)S(1)} all-reduce(f32[2048]{0:T(1024)S(1)} %get-tuple-element.26), channel_id=1, replica_groups=mesh['section'=2,'seq'=16,'tensor'=8] {'tensor'}, use_global_device_ids=true, to_apply=%region_5.6 | all-reduce | flops 2048 | bytes 16384 | tf_op jit(solution)/shard_map/psum | solution.py:152
  424.0 4.2 all-to-all-start.14
  428.2 2.7 fusion.21
  430.9 2.6 copy.116
  433.5 20.5 %all-to-all-done.14 = bf16[8,32,2048]{2,1,0:T(8,128)(2,1)} async-done(((bf16[8,32,2048]{2,1,0:T(8,128)(2,1)}), bf16[8,32,2048]{2,1,0:T(8,128)(2,1)}, u32[]{:S(2)}, u32[]{:S(2)}) %all-to-all-start.14) | async-done | bytes 1048608 | tf_op jit(solution)/shard_map/all_to_all | solution.py:46
  454.0 6.9 all-to-all-start.12
  460.9 2.7 convolution_convert_fusion.2
  463.6 11.3 %all-to-all-done.12 = bf16[8,256,256]{2,0,1:T(8,128)(2,1)} async-done(((bf16[8,256,256]{2,0,1:T(8,128)(2,1)}), bf16[8,256,256]{2,0,1:T(8,128)(2,1)}, u32[]{:S(2)}, u32[]{:S(2)}) %all-to-all-start.12) | async-done | bytes 1048608 | tf_op jit(solution)/shard_map/all_to_all | solution.py:89
  474.8 4.2 all-to-all-start.15
  482.2 2.7 copy.120
  484.8 18.1 %all-to-all-done.15 = bf16[8,32,2048]{2,1,0:T(8,128)(2,1)} async-done(((bf16[8,32,2048]{2,1,0:T(8,128)(2,1)}), bf16[8,32,2048]{2,1,0:T(8,128)(2,1)}, u32[]{:S(2)}, u32[]{:S(2)}) %all-to-all-start.15) | async-done | bytes 1048608 | tf_op jit(solution)/shard_map/all_to_all | solution.py:50
  502.9 4.7 all-to-all-start.13
  510.9 10.4 %reshape.483 = f32[8,16,16,256]{2,1,0,3:T(8,128)} reshape(f32[2048,4,8,8]{0,3,2,1:T(8,128)} %copy.121) | data formatting | bytes 4194304 | tf_op jit(solution)/shard_map/div | solution.py:158
  521.3 12.9 %copy.122 = f32[8,16,16,256]{3,2,0,1:T(8,128)} copy(f32[8,16,16,256]{2,1,0,3:T(8,128)} %reshape.483) | data formatting | bytes 4194304 | tf_op jit(solution)/shard_map/div | solution.py:158
  537.9 4.2 all-to-all-start.16
  545.1 6.3 slice.28
  552.8 32.3 %all_gather.18 = bf16[16,2048]{1,0:T(8,128)(2,1)} all-gather(bf16[16,256]{1,0:T(8,128)(2,1)S(1)} %reshape.465), channel_id=1, replica_groups=mesh['section'=2,'seq'=16,'tensor'=8] {'tensor'}, dimensions={1}, use_global_device_ids=true | all-gather | bytes 73728 | tf_op jit(solution)/shard_map/all_gather | solution.py:165
  585.2 2.7 convolution_convert_fusion
  587.9 5.8 all-to-all-start.17
  597.3 34.9 %all_gather.20 = bf16[16,2048]{1,0:T(8,128)(2,1)} all-gather(bf16[16,256]{1,0:T(8,128)(2,1)S(1)} %reshape.467), channel_id=1, replica_groups=mesh['section'=2,'seq'=16,'tensor'=8] {'tensor'}, dimensions={1}, use_global_device_ids=true | all-gather | bytes 73728 | tf_op jit(solution)/shard_map/all_gather | solution.py:165
  639.8 26.5 %all_gather.22 = bf16[16,2048]{1,0:T(8,128)(2,1)} all-gather(bf16[16,256]{1,0:T(8,128)(2,1)S(1)} %reshape.469), channel_id=1, replica_groups=mesh['section'=2,'seq'=16,'tensor'=8] {'tensor'}, dimensions={1}, use_global_device_ids=true | all-gather | bytes 73728 | tf_op jit(solution)/shard_map/all_gather | solution.py:165
  671.2 11.6 %all-gather.6.cloned.1.call-done = bf16[256,2048]{1,0:T(8,128)(2,1)} async-done(((bf16[16,2048]{1,0:T(8,128)(2,1)}), bf16[256,2048]{1,0:T(8,128)(2,1)}) %all-gather.6.cloned.1.call-update) | async-done | bytes 1048592 | tf_op jit(solution)/shard_map/all_gather | solution.py:167
  682.8 2.9 fusion.34
  687.4 4.0 copy.129
  691.4 40.9 %all-gather.8.cloned.1.call-done = bf16[256,2048]{1,0:T(8,128)(2,1)} async-done(((bf16[16,2048]{1,0:T(8,128)(2,1)}), bf16[256,2048]{1,0:T(8,128)(2,1)}) %all-gather.8.cloned.1.call-update) | async-done | bytes 1048592 | tf_op jit(solution)/shard_map/all_gather | solution.py:167
  734.1 17.7 %all-reduce.1 = (f32[256]{0:T(256)S(1)}, f32[256]{0:T(256)S(1)}, f32[256]{0:T(256)S(1)}, f32[256]{0:T(256)S(1)}, f32[256]{0:T(256)S(1)}, /*index=5*/f32[256]{0:T(256)S(1)}) all-reduce(f32[256]{0:T(256)S(1)} %get-tuple-element.36, f32[256]{0:T(256)S(1)} %get-tuple-element.37, ...), channel_id=1, replica_groups=mesh['section'=2,'seq'=16,'tensor'=8] {'tensor'}, use_global_device_ids=true, to_apply=%region_16.17 | all-reduce | flops 1536 | bytes 12288 | tf_op jit(solution)/shard_map/psum | solution.py:175
  751.8 38.6 %all-reduce = (f32[256]{0:T(256)S(1)}, f32[256]{0:T(256)S(1)}, f32[256]{0:T(256)S(1)}, f32[256]{0:T(256)S(1)}, f32[256]{0:T(256)S(1)}, /*index=5*/f32[256]{0:T(256)S(1)}) all-reduce(f32[256]{0:T(256)S(1)} %get-tuple-element.20, f32[256]{0:T(256)S(1)} %get-tuple-element.21, ...), channel_id=1, replica_groups=mesh['section'=2,'seq'=16,'tensor'=8] {'seq'}, use_global_device_ids=true, to_apply=%region_17.18 | all-reduce | flops 1536 | bytes 12288 | tf_op jit(solution)/shard_map/psum | solution.py:175
  (153 shorter events, 82.7 us)
Async XLA Ops:
  7.2 31.8 %copy-start = (bf16[1,8,256,256]{3,2,1,0:T(8,128)(2,1)S(1)}, bf16[1,8,256,256]{3,2,1,0:T(8,128)(2,1)}, u32[]{:S(2)}) copy-start(bf16[1,8,256,256]{3,2,1,0:T(8,128)(2,1)} %param.12) | copy-start | bytes 3145732
  9.6 22.2 %copy-start.19 = (bf16[256,256]{1,0:T(8,128)(2,1)}, bf16[256,256]{1,0:T(8,128)(2,1)S(1)}, u32[]{:S(2)}) copy-start(bf16[256,256]{1,0:T(8,128)(2,1)S(1)} %mul.236) | copy-start | bytes 393220
  12.3 19.5 %copy-start.26 = (f32[1,256]{1,0:T(1,128)S(1)}, f32[1,256]{1,0:T(1,128)}, u32[]{:S(2)}) copy-start(f32[1,256]{1,0:T(1,128)} %param.11) | copy-start | bytes 3076
  12.9 24.6 %copy-start.1 = (bf16[1,2048,256]{1,2,0:T(8,128)(2,1)}, bf16[1,2048,256]{1,2,0:T(8,128)(2,1)S(1)}, u32[]{:S(2)}) copy-start(bf16[1,2048,256]{1,2,0:T(8,128)(2,1)S(1)} %copy.135) | copy-start | bytes 3145732
  33.3 29.7 %all-to-all-start.2 = ((bf16[8,32,2048]{2,1,0:T(8,128)(2,1)}), bf16[8,32,2048]{2,1,0:T(8,128)(2,1)}, u32[]{:S(2)}, u32[]{:S(2)}) async-start(bf16[8,32,2048]{2,1,0:T(8,128)(2,1)} %bitcast.21), calls=%async_computation.2 | async-start | bytes 2097152 | tf_op jit(solution)/shard_map/all_to_all | solution.py:46
  38.6 1.8 copy-start.3
  40.4 29.7 %copy-start.24 = (bf16[1,64,32,32]{1,3,2,0:T(8,128)(2,1)S(1)}, bf16[1,64,32,32]{1,3,2,0:T(8,128)(2,1)}, u32[]{:S(2)}) copy-start(bf16[1,64,32,32]{1,3,2,0:T(8,128)(2,1)} %param.15) | copy-start | bytes 393220
  43.1 27.0 %copy-start.25 = (bf16[1,64,32,32]{1,3,2,0:T(8,128)(2,1)S(1)}, bf16[1,64,32,32]{1,3,2,0:T(8,128)(2,1)}, u32[]{:S(2)}) copy-start(bf16[1,64,32,32]{1,3,2,0:T(8,128)(2,1)} %param.17) | copy-start | bytes 393220
  63.0 20.9 %all-to-all-start = ((bf16[8,256,256]{2,0,1:T(8,128)(2,1)}), bf16[8,256,256]{2,0,1:T(8,128)(2,1)}, u32[]{:S(2)}, u32[]{:S(2)}) async-start(bf16[8,256,256]{2,0,1:T(8,128)(2,1)} %copy.92), calls=%async_computation | async-start | bytes 2097152 | tf_op jit(solution)/shard_map/all_to_all | solution.py:89
  84.0 5.2 copy-start.14
  84.0 27.3 %all-to-all-start.3 = ((bf16[8,32,2048]{2,1,0:T(8,128)(2,1)}), bf16[8,32,2048]{2,1,0:T(8,128)(2,1)S(1)}, u32[]{:S(2)}, u32[]{:S(2)}) async-start(bf16[8,32,2048]{2,1,0:T(8,128)(2,1)} %bitcast.247), calls=%async_computation.3 | async-start | bytes 2097152 | tf_op jit(solution)/shard_map/all_to_all | solution.py:50
  90.7 25.6 %copy-start.22 = (bf16[64,4,4,64]{3,2,1,0:T(4,128)(2,1)S(1)}, bf16[64,4,4,64]{3,2,1,0:T(4,128)(2,1)}, u32[]{:S(2)}) copy-start(bf16[64,4,4,64]{3,2,1,0:T(4,128)(2,1)} %get-tuple-element.41) | copy-start | bytes 393220
  111.2 26.8 %all-to-all-start.1 = ((bf16[128,16,256]{2,1,0:T(8,128)(2,1)}), bf16[128,16,256]{2,1,0:T(8,128)(2,1)}, u32[]{:S(2)}, u32[]{:S(2)}) async-start(bf16[128,16,256]{2,1,0:T(8,128)(2,1)} %copy.96), calls=%async_computation.1 | async-start | bytes 2097152 | tf_op jit(solution)/shard_map/all_to_all | solution.py:92
  139.7 5.7 copy-start.13
  141.1 30.0 %all-to-all-start.4 = ((bf16[8,32,2048]{2,1,0:T(8,128)(2,1)}), bf16[8,32,2048]{2,1,0:T(8,128)(2,1)}, u32[]{:S(2)}, u32[]{:S(2)}) async-start(bf16[8,32,2048]{2,1,0:T(8,128)(2,1)} %bitcast.250), calls=%async_computation.4 | async-start | bytes 2097152 | tf_op jit(solution)/shard_map/all_to_all | solution.py:66
  201.2 1.2 copy-start.2
  203.7 4.5 collective-permute-start
  225.8 2.5 copy-start.20
  227.4 1.0 copy-start.6
  229.8 29.8 %all-to-all-start.8 = ((bf16[8,32,2048]{2,1,0:T(8,128)(2,1)}), bf16[8,32,2048]{2,1,0:T(8,128)(2,1)}, u32[]{:S(2)}, u32[]{:S(2)}) async-start(bf16[8,32,2048]{2,1,0:T(8,128)(2,1)} %bitcast.251), calls=%async_computation.8 | async-start | bytes 2097152 | tf_op jit(solution)/shard_map/all_to_all | solution.py:46
  259.6 20.8 %all-to-all-start.6 = ((bf16[8,256,256]{2,0,1:T(8,128)(2,1)}), bf16[8,256,256]{2,0,1:T(8,128)(2,1)}, u32[]{:S(2)}, u32[]{:S(2)}) async-start(bf16[8,256,256]{2,0,1:T(8,128)(2,1)} %copy.106), calls=%async_computation.6 | async-start | bytes 2097152 | tf_op jit(solution)/shard_map/all_to_all | solution.py:89
  280.4 27.9 %all-to-all-start.9 = ((bf16[8,32,2048]{2,1,0:T(8,128)(2,1)}), bf16[8,32,2048]{2,1,0:T(8,128)(2,1)}, u32[]{:S(2)}, u32[]{:S(2)}) async-start(bf16[8,32,2048]{2,1,0:T(8,128)(2,1)} %bitcast.248), calls=%async_computation.9 | async-start | bytes 2097152 | tf_op jit(solution)/shard_map/all_to_all | solution.py:50
  284.6 1.6 copy-start.15
  308.3 31.3 %all-to-all-start.7 = ((bf16[128,16,256]{2,1,0:T(8,128)(2,1)}), bf16[128,16,256]{2,1,0:T(8,128)(2,1)}, u32[]{:S(2)}, u32[]{:S(2)}) async-start(bf16[128,16,256]{2,1,0:T(8,128)(2,1)} %copy.110), calls=%async_computation.7 | async-start | bytes 2097152 | tf_op jit(solution)/shard_map/all_to_all | solution.py:92
  398.5 1.2 copy-start.9
  399.7 3.9 copy-start.7
  400.0 5.0 copy-start.10
  400.0 3.6 collective-permute-start.1
  420.0 2.5 copy-start.21
  421.6 1.0 copy-start.5
  424.0 30.1 %all-to-all-start.14 = ((bf16[8,32,2048]{2,1,0:T(8,128)(2,1)}), bf16[8,32,2048]{2,1,0:T(8,128)(2,1)}, u32[]{:S(2)}, u32[]{:S(2)}) async-start(bf16[8,32,2048]{2,1,0:T(8,128)(2,1)} %bitcast.249), calls=%async_computation.14 | async-start | bytes 2097152 | tf_op jit(solution)/shard_map/all_to_all | solution.py:46
  454.0 20.8 %all-to-all-start.12 = ((bf16[8,256,256]{2,0,1:T(8,128)(2,1)}), bf16[8,256,256]{2,0,1:T(8,128)(2,1)}, u32[]{:S(2)}, u32[]{:S(2)}) async-start(bf16[8,256,256]{2,0,1:T(8,128)(2,1)} %copy.116), calls=%async_computation.12 | async-start | bytes 2097152 | tf_op jit(solution)/shard_map/all_to_all | solution.py:89
  474.8 28.1 %all-to-all-start.15 = ((bf16[8,32,2048]{2,1,0:T(8,128)(2,1)}), bf16[8,32,2048]{2,1,0:T(8,128)(2,1)}, u32[]{:S(2)}, u32[]{:S(2)}) async-start(bf16[8,32,2048]{2,1,0:T(8,128)(2,1)} %bitcast.246), calls=%async_computation.15 | async-start | bytes 2097152 | tf_op jit(solution)/shard_map/all_to_all | solution.py:50
  479.1 1.6 copy-start.16
  502.9 31.3 %all-to-all-start.13 = ((bf16[128,16,256]{2,1,0:T(8,128)(2,1)}), bf16[128,16,256]{2,1,0:T(8,128)(2,1)}, u32[]{:S(2)}, u32[]{:S(2)}) async-start(bf16[128,16,256]{2,1,0:T(8,128)(2,1)} %copy.120), calls=%async_computation.13 | async-start | bytes 2097152 | tf_op jit(solution)/shard_map/all_to_all | solution.py:92
  537.9 47.3 %all-to-all-start.16 = ((bf16[8,32,2048]{2,1,0:T(8,128)(2,1)}), bf16[8,32,2048]{2,1,0:T(8,128)(2,1)}, u32[]{:S(2)}, u32[]{:S(2)}) async-start(bf16[8,32,2048]{2,1,0:T(8,128)(2,1)} %bitcast.244), calls=%async_computation.16 | async-start | bytes 2097152 | tf_op jit(solution)/shard_map/all_to_all | solution.py:66
  542.2 126.7 %all-gather.4.cloned.1.call-start = ((), (), s32[]{:S(2)}) async-start(), calls=%async_computation.18 | async-start | bytes 1114112 | tf_op jit(solution)/shard_map/all_gather | solution.py:167
  542.2 1.6 copy-start.4
  587.9 44.4 %all-to-all-start.17 = ((bf16[8,32,2048]{2,1,0:T(8,128)(2,1)}), bf16[8,32,2048]{2,1,0:T(8,128)(2,1)}, u32[]{:S(2)}, u32[]{:S(2)}) async-start(bf16[8,32,2048]{2,1,0:T(8,128)(2,1)} %bitcast.245), calls=%async_computation.17 | async-start | bytes 2097152 | tf_op jit(solution)/shard_map/all_to_all | solution.py:70
  593.6 89.2 %all-gather.6.cloned.1.call-start = ((), (), s32[]{:S(2)}) async-start(), calls=%async_computation.19 | async-start | bytes 1114112 | tf_op jit(solution)/shard_map/all_gather | solution.py:167
  632.2 100.1 %all-gather.8.cloned.1.call-start = ((), (), s32[]{:S(2)}) async-start(), calls=%async_computation.20 | async-start | bytes 1114112 | tf_op jit(solution)/shard_map/all_gather | solution.py:167
  633.7 1.2 copy-start.8
  636.2 30.1 %copy-start.27 = (s32[2,256]{1,0:T(2,128)S(1)}, s32[2,256]{1,0:T(2,128)}, u32[]{:S(2)}) copy-start(s32[2,256]{1,0:T(2,128)} %param.19) | copy-start | bytes 6148
  668.9 16.8 %copy-start.11 = (bf16[2048,256]{0,1:T(8,128)(2,1)S(1)}, bf16[2048,256]{0,1:T(8,128)(2,1)}, u32[]{:S(2)}) copy-start(bf16[2048,256]{0,1:T(8,128)(2,1)} %copy-done.10) | copy-start | bytes 3145732
  668.9 16.8 %copy-start.12 = (bf16[2048,256]{0,1:T(8,128)(2,1)S(1)}, bf16[2048,256]{0,1:T(8,128)(2,1)}, u32[]{:S(2)}) copy-start(bf16[2048,256]{0,1:T(8,128)(2,1)} %fusion.7) | copy-start | bytes 3145732
  682.8 2.9 copy-start.18
  687.4 44.9 %copy-start.17 = (bf16[1,2048,256]{2,1,0:T(8,128)(2,1)S(1)}, bf16[1,2048,256]{2,1,0:T(8,128)(2,1)}, u32[]{:S(2)}) copy-start(bf16[1,2048,256]{2,1,0:T(8,128)(2,1)} %param.18) | copy-start | bytes 3145732
  687.4 44.9 %copy-start.23 = (f32[256,256]{0,1:T(8,128)S(1)}, f32[256,256]{0,1:T(8,128)}, u32[]{:S(2)}) copy-start(f32[256,256]{0,1:T(8,128)} %fusion.34) | copy-start | bytes 786436
Sparse Core Ops, SparseCore 0:
  585.3 47.9 all-gather.3
  635.8 47.0 all-gather.5
  685.2 47.0 all-gather.7
